TPU v7x, 256 devices: a whole 4x4x8 slice. The times are simulated.
256 devices in a mesh: dp: 2 (over z_lo), tensor: 128 (over x, y, z_hi, core).
Axes of the slice: x: 4, y: 4, z: 8 (z_hi: 4, z_lo: 2; z = z_hi * 2 + z_lo), core: 2. Of those that a mesh axis runs over, the one named last changes fastest.
Arguments:
- tokens: bfloat16 [2, 16384, 4096], P('dp', 'tensor'), may hold values from -35 to 35
- norm_gain: float32 [4096], replicated, may hold values from 0.1 to 1.9
- segments: int32 [2, 16384], P('dp', 'tensor'), may hold values from 0 to 7, never falling along the last dimension, each value on 1 to 8192 neighbouring positions
- deal_table: int32 [128, 2], P('tensor'), may hold values from 0 to 1, each once within a row
- projection: bfloat16 [32768, 768], P('tensor'), may hold values from -1 to 1
Outputs:
- context: bfloat16 [2, 16384, 4096], P('dp', 'tensor')
- key_cache: bfloat16 [2, 8, 16384, 128], P('dp', None, 'tensor')
- value_cache: bfloat16 [2, 8, 16384, 128], P('dp', None, 'tensor')
Inputs may be any that keep to these rules, and one draw needn't show every extreme that they name: `segments`: segment ids never fall along a buffer; every id appears, each on at most 8192 positions, one on exactly 8192. `deal_table`: each row names every group once.
All inputs are finite; a program needn't handle non-finite values.
Results may differ from a plain program's by a relative error of at most 0.0082.
Values may be sent and summed in bfloat16 or wider, within the bound.
A program may use at most 128 MiB of HBM per device.

v0:
```python
import jax
import jax.numpy as jnp
from jax import lax
from jax.sharding import PartitionSpec as P

QUERY_HEADS = 32
KEY_VALUE_HEADS = 8
HEAD_SIZE = 128
NSEG = 8
WINDOW = 512
SINKS = 4
rope_base = 500000.0
norm_eps = 1e-05


def from_partner(value, axis, apart):
    mask = 2**apart
    pairs = [(source, source ^ mask) for source in range(lax.axis_size(axis))]
    return lax.ppermute(value, axis, pairs)


def shifted(block, axis, distance):
    devices = range(lax.axis_size(axis))
    route = [(i - distance, i) for i in devices if i - distance in devices]
    return lax.ppermute(block, axis, route)


def stack_pair(holding, arrived, upper_flag, axis_pos):
    lower_part = jnp.where(upper_flag, arrived, holding)
    upper_part = jnp.where(upper_flag, holding, arrived)
    return jnp.stack((lower_part, upper_part), axis=axis_pos)


def rotary(values, angles):
    half_width = values.shape[-1] // 2
    first_half = values[..., :half_width]
    second_half = values[..., half_width:]
    cosine = jnp.cos(angles)
    sine_part = jnp.sin(angles)
    return jnp.concatenate(
        (
            first_half * cosine - second_half * sine_part,
            second_half * cosine + first_half * sine_part,
        ),
        -1,
    )


def body(tokens, norm_gain, segments, deal_table, projection):
    group_id = lax.axis_index("dp")
    device_number = lax.axis_index("tensor")
    tensor_width = lax.axis_size("tensor")
    token_per_device = tokens.shape[1]
    model_width = tokens.shape[2]
    block_length = KEY_VALUE_HEADS * token_per_device
    head_number = device_number % KEY_VALUE_HEADS
    block_number = device_number // KEY_VALUE_HEADS
    group_queries = QUERY_HEADS // KEY_VALUE_HEADS
    head_bit_flags = KEY_VALUE_HEADS.bit_length() - 1
    level_bits = tensor_width.bit_length() - 1
    own_page = tokens[0]
    other_page = from_partner(own_page, "dp", 0)
    owner_group = jnp.sum(jnp.where(jnp.arange(deal_table.shape[1]) == group_id, deal_table[0], 0))
    stay_here = owner_group == group_id
    dealt_rows = jnp.where(stay_here, own_page, other_page)
    widened = dealt_rows.astype(jnp.float32)
    normed = (
        widened * lax.rsqrt(jnp.mean(widened * widened, -1, keepdims=True) + norm_eps) * norm_gain
    ).astype(jnp.bfloat16)
    segment_ids = segments[0]
    segment_match = segment_ids[:, None] == jnp.arange(NSEG)[None, :]
    counts_total = lax.psum(jnp.sum(segment_match.astype(jnp.float32), 0), "tensor")
    counts_int = counts_total.astype(jnp.int32)
    seg_starts = jnp.cumsum(counts_int) - counts_int
    row_starts = jnp.sum(jnp.where(segment_match, seg_starts[None, :], 0), 1)
    bit_order = list(range(head_bit_flags))
    rows_held = normed
    starts_held = row_starts
    gathered_bits = []
    for bit_index in bit_order:
        upper_flag = device_number >> bit_index & 1 == 1
        axis_pos = len([earlier for earlier in gathered_bits if earlier > bit_index])
        rows_far = from_partner(rows_held, "tensor", bit_index)
        starts_far = from_partner(starts_held, "tensor", bit_index)
        rows_held = stack_pair(rows_held, rows_far, upper_flag, axis_pos)
        starts_held = stack_pair(starts_held, starts_far, upper_flag, axis_pos)
        gathered_bits.append(bit_index)
    rows_block = rows_held.reshape(block_length, model_width)
    starts_block = starts_held.reshape(block_length)
    weights_held = projection
    for level_index in range(level_bits - head_bit_flags):
        bit_index = head_bit_flags + level_index
        upper_flag = device_number >> bit_index & 1 == 1
        arrived = from_partner(weights_held, "tensor", bit_index)
        weights_held = stack_pair(weights_held, arrived, upper_flag, 0).reshape(
            -1, weights_held.shape[1]
        )
    projected = jnp.dot(rows_block, weights_held, preferred_element_type=jnp.float32)
    rope_freq = rope_base ** (-(jnp.arange(0, HEAD_SIZE, 2).astype(jnp.float32) / HEAD_SIZE))
    block_positions = block_number * block_length + jnp.arange(block_length)
    angles = (block_positions - starts_block).astype(jnp.float32)[:, None] * rope_freq[None, :]
    queries = rotary(
        projected[:, : group_queries * HEAD_SIZE].reshape(block_length, group_queries, HEAD_SIZE),
        angles[:, None, :],
    ).astype(jnp.bfloat16)
    keys_own = rotary(
        projected[:, group_queries * HEAD_SIZE : (group_queries + 1) * HEAD_SIZE], angles
    ).astype(jnp.bfloat16)
    values_own = projected[:, (group_queries + 1) * HEAD_SIZE :].astype(jnp.bfloat16)
    local_pairs = jnp.concatenate((keys_own, values_own), 1)
    reach_blocks = -(-WINDOW // block_length)
    previous_pairs = [shifted(local_pairs, "tensor", 1 * KEY_VALUE_HEADS)]
    window_pairs = jnp.concatenate(previous_pairs + [local_pairs], 0)
    sink_positions = (seg_starts[:, None] + jnp.arange(SINKS)[None, :]).reshape(NSEG * SINKS)
    local_rows = sink_positions - block_number * block_length
    selector = (local_rows[:, None] == jnp.arange(block_length)[None, :]).astype(jnp.bfloat16)
    selected_rows = jnp.dot(selector, rows_block, preferred_element_type=jnp.float32)
    slice_width = model_width // KEY_VALUE_HEADS
    own_slice = jnp.arange(model_width) // slice_width == head_number
    slice_rows = jnp.where(own_slice[None, :], selected_rows, 0.0)
    sink_table = lax.psum(slice_rows, "tensor")
    sink_normed = sink_table.astype(jnp.bfloat16)
    sink_projected = jnp.dot(
        sink_normed,
        weights_held[:, group_queries * HEAD_SIZE :],
        preferred_element_type=jnp.float32,
    ).reshape(NSEG, SINKS, 2 * HEAD_SIZE)
    sink_angles = jnp.arange(SINKS).astype(jnp.float32)[:, None] * rope_freq[None, :]
    sink_key_rows = rotary(sink_projected[:, :, :HEAD_SIZE], sink_angles[None, :, :]).astype(
        jnp.bfloat16
    )
    sink_value_rows = sink_projected[:, :, HEAD_SIZE:].astype(jnp.bfloat16)
    sink_pairs = jnp.concatenate((sink_key_rows, sink_value_rows), -1)
    tile_rows = min(512, block_length)
    score_scale = HEAD_SIZE ** (-0.5)

    def attend(tile_start):
        query_tile = lax.dynamic_slice_in_dim(queries, tile_start, tile_rows, 0)
        query_pos = block_number * block_length + tile_start + jnp.arange(tile_rows)
        query_start = lax.dynamic_slice_in_dim(starts_block, tile_start, tile_rows, 0)
        key_from = reach_blocks * block_length + tile_start - WINDOW
        key_pairs = lax.dynamic_slice_in_dim(window_pairs, key_from, WINDOW + tile_rows, 0)
        key_pos = (
            (block_number - reach_blocks) * block_length + key_from + jnp.arange(WINDOW + tile_rows)
        )
        scores = (
            jnp.einsum(
                "rgd,kd->rgk",
                query_tile,
                key_pairs[:, :HEAD_SIZE],
                preferred_element_type=jnp.float32,
            )
            * score_scale
        )
        allowed = (
            (key_pos[None, :] <= query_pos[:, None])
            & (key_pos[None, :] >= query_start[:, None])
            & (key_pos[None, :] >= query_pos[:, None] - WINDOW)
        )
        chooser = (seg_starts[None, :] == query_start[:, None]).astype(jnp.bfloat16)
        row_sinks = jnp.einsum(
            "rs,sqc->rqc", chooser, sink_pairs, preferred_element_type=jnp.float32
        ).astype(jnp.bfloat16)
        sink_scores = (
            jnp.einsum(
                "rgd,rqd->rgq",
                query_tile,
                row_sinks[:, :, :HEAD_SIZE],
                preferred_element_type=jnp.float32,
            )
            * score_scale
        )
        sink_pos = query_start[:, None] + jnp.arange(SINKS)[None, :]
        sink_allowed = (sink_pos <= query_pos[:, None]) & (sink_pos < query_pos[:, None] - WINDOW)
        masked = jnp.where(allowed[:, None, :], scores, -jnp.inf)
        masked_sinks = jnp.where(sink_allowed[:, None, :], sink_scores, -jnp.inf)
        top_score = jnp.maximum(
            jnp.max(masked, -1, keepdims=True), jnp.max(masked_sinks, -1, keepdims=True)
        )
        window_weights = jnp.exp(masked - top_score)
        sink_weights = jnp.exp(masked_sinks - top_score)
        denominator = jnp.sum(window_weights, -1, keepdims=True) + jnp.sum(
            sink_weights, -1, keepdims=True
        )
        window_probs = (window_weights / denominator).astype(jnp.bfloat16)
        sink_probs = (sink_weights / denominator).astype(jnp.bfloat16)
        mixed_rows = jnp.einsum(
            "rgk,kd->rgd",
            window_probs,
            key_pairs[:, HEAD_SIZE:],
            preferred_element_type=jnp.float32,
        )
        mixed_rows = mixed_rows + jnp.einsum(
            "rgq,rqd->rgd",
            sink_probs,
            row_sinks[:, :, HEAD_SIZE:],
            preferred_element_type=jnp.float32,
        )
        return mixed_rows.astype(jnp.bfloat16).reshape(tile_rows, group_queries * HEAD_SIZE)

    tile_offsets = jnp.arange(block_length // tile_rows, dtype=jnp.int32) * tile_rows
    context_block = lax.map(attend, tile_offsets).reshape(block_length, group_queries * HEAD_SIZE)
    pairs_by_dest = local_pairs.reshape((2,) * head_bit_flags + (token_per_device, 2 * HEAD_SIZE))
    context_by_dest = context_block.reshape(
        (2,) * head_bit_flags + (token_per_device, group_queries * HEAD_SIZE)
    )
    kept_pairs = pairs_by_dest
    for bit_index in range(head_bit_flags):
        axis_pos = head_bit_flags - 1 - bit_index
        bit_value = device_number >> bit_index & 1
        own_half = lax.dynamic_index_in_dim(kept_pairs, bit_value, axis_pos, keepdims=False)
        sent_half = lax.dynamic_index_in_dim(kept_pairs, 1 - bit_value, axis_pos, keepdims=False)
        arrived = from_partner(sent_half, "tensor", bit_index)
        kept_pairs = stack_pair(own_half, arrived, bit_value == 1, axis_pos)
    kept_context = context_by_dest
    for bit_index in range(head_bit_flags):
        axis_pos = head_bit_flags - 1 - bit_index
        bit_value = device_number >> bit_index & 1
        own_half = lax.dynamic_index_in_dim(kept_context, bit_value, axis_pos, keepdims=False)
        sent_half = lax.dynamic_index_in_dim(kept_context, 1 - bit_value, axis_pos, keepdims=False)
        arrived = from_partner(sent_half, "tensor", bit_index)
        kept_context = stack_pair(own_half, arrived, bit_value == 1, axis_pos)
    cached_heads = kept_pairs.reshape(KEY_VALUE_HEADS, token_per_device, 2 * HEAD_SIZE)
    key_cache = cached_heads[:, :, :HEAD_SIZE][None]
    value_cache = cached_heads[:, :, HEAD_SIZE:][None]
    context_local = (
        kept_context.reshape(KEY_VALUE_HEADS, token_per_device, group_queries * HEAD_SIZE)
        .transpose(1, 0, 2)
        .reshape(token_per_device, QUERY_HEADS * HEAD_SIZE)
    )
    context_back = from_partner(context_local, "dp", 0)
    context = jnp.where(stay_here, context_local, context_back)[None]
    return (context, key_cache, value_cache)


def solution(mesh):
    placed = (P("dp", "tensor", None), P(), P("dp", "tensor"), P("tensor", None), P("tensor", None))
    return jax.shard_map(
        body,
        mesh=mesh,
        in_specs=placed,
        out_specs=(
            P("dp", "tensor", None),
            P("dp", None, "tensor", None),
            P("dp", None, "tensor", None),
        ),
        check_vma=False,
    )
```

profile of v0, /device:TPU:32, one launch (start us, length us, event | category | flops | bytes accessed | tf_op | source)
XLA Modules:
  0.0 1571.1 jit_solution(10747229112647004159)
XLA Ops:
  0.7 1.9 collective-permute-start.3
  4.5 7.4 collective-permute-done.7
  13.0 3.3 collective-permute-start.8
  16.3 9.5 collective-permute-done.3
  26.8 1.6 fusion.25
  28.6 4.5 collective-permute-done.8
  34.5 1.6 collective-permute-start.9
  36.1 1.7 select_bitcast_fusion.10
  40.3 3.3 collective-permute-start.5
  43.6 25.5 %collective-permute-done.9 = bf16[1024,768]{1,0:T(8,128)(2,1)} collective-permute-done((bf16[1024,768]{1,0:T(8,128)(2,1)S(1)}, bf16[1024,768]{1,0:T(8,128)(2,1)}, u32[]{:S(2)}, u32[]{:S(2)}) %collective-permute-start.9) | collective-permute-done | bytes 1572896 | tf_op jit(solution)/shard_map/ppermute | solution.py:19
  70.7 1.9 pad_maximum_fusion.3
  72.6 3.1 collective-permute-start.10
  75.8 56.0 %collective-permute-done.5 = bf16[2,128,4096]{2,1,0:T(8,128)(2,1)} collective-permute-done((bf16[2,128,4096]{2,1,0:T(8,128)(2,1)}, bf16[2,128,4096]{2,1,0:T(8,128)(2,1)}, u32[]{:S(2)}, u32[]{:S(2)}) %collective-permute-start.5) | collective-permute-done | bytes 2097184 | tf_op jit(solution)/shard_map/ppermute | solution.py:19
  131.7 2.0 select_bitcast_fusion.5
  133.8 2.6 pad_maximum_fusion.2
  136.4 4.6 collective-permute-start.6
  141.1 513.5 %psum.14 = f32[8]{0:T(128)S(1)} all-reduce(f32[8]{0:T(128)S(1)} %convert_reduce_fusion), channel_id=1, replica_groups=mesh['dp'=2,'tensor'=128] {'tensor'}, use_global_device_ids=true, to_apply=%region_3.4 | all-reduce | flops 8 | bytes 64 | tf_op jit(solution)/shard_map/psum | solution.py:72
  658.0 4.4 collective-permute-done.1
  663.4 6.9 collective-permute-done.2
  672.1 3.3 select_bitcast_fusion.3
  675.4 3.2 pad_maximum_fusion.1
  678.6 5.1 select_bitcast_fusion.1
  683.8 7.6 pad_maximum_fusion
  691.4 11.3 fusion.60
  702.7 2.3 convolution_select_fusion
  705.0 684.3 %all-reduce.1 = bf16[32,4096]{1,0:T(8,128)(2,1)S(1)} all-reduce(f32[32,4096]{1,0:T(8,128)} %convolution_select_fusion), channel_id=1, replica_groups=mesh['dp'=2,'tensor'=128] {'tensor'}, use_global_device_ids=true, to_apply=%region_6.7 | all-reduce | flops 131072 | bytes 786432 | tf_op jit(solution)/shard_map/psum | solution.py:121
  1389.3 2.0 fusion.26
  1392.3 2.6 subtract_convert_fusion.1
  1396.4 2.1 collective-permute-start.11
  1399.6 1.8 copy.242
  1401.5 2.0 copy.243
  1407.3 2.1 subtract_convert_fusion
  1411.0 2.1 maximum_maximum_fusion
  1413.2 57.3 %while.15 = (s32[]{:T(128)}, bf16[2,512,512]{2,1,0:T(8,128)(2,1)}, s32[2]{0:T(128)}, s32[]{:T(128)}, s32[]{:T(128)}, /*index=5*/s32[1024]{0:T(1024)}, bf16[1024,...) while((s32[]{:T(128)}, bf16[2,512,512]{2,1,0:T(8,128)(2,1)}, ...), condition=%wide.region_12.13_spmd, body=%wide.region_7.12_spmd.sunk | while | flops 1115269120 | bytes 41343824 | solution.py:202
  1422.2 5.9 fusion.93
  1429.4 4.7 fusion.96
  1435.5 5.2 fusion.99
  1450.9 5.9 fusion.93
  1458.0 4.7 fusion.96
  1464.2 5.2 fusion.99
  1471.6 1.9 collective-permute-done.12
  1478.9 17.6 %collective-permute-done.13 = bf16[2,2,128,512]{3,2,1,0:T(8,128)(2,1)S(1)} collective-permute-done((bf16[2,2,128,512]{3,2,1,0:T(8,128)(2,1)S(1)}, bf16[2,2,128,512]{3,2,1,0:T(8,128)(2,1)S(1)}, u32[]{:S(2)}, u32[]{:S(2)}) %collective-permute-start.13) | collective-permute-done | bytes 524320 | tf_op jit(solution)/shard_map/ppermute | solution.py:19
  1499.0 3.3 collective-permute-start.17
  1502.3 19.0 %collective-permute-done.14 = bf16[2,2,128,512]{3,2,1,0:T(8,128)(2,1)S(1)} collective-permute-done((bf16[2,2,128,512]{3,2,1,0:T(8,128)(2,1)S(1)}, bf16[2,2,128,512]{3,2,1,0:T(8,128)(2,1)S(1)}, u32[]{:S(2)}, u32[]{:S(2)}) %collective-permute-start.14) | collective-permute-done | bytes 524320 | tf_op jit(solution)/shard_map/ppermute | solution.py:19
  1522.8 6.4 collective-permute-start.15
  1529.1 4.3 collective-permute-done.17
  1534.4 2.9 collective-permute-start.18
  1537.3 31.6 %collective-permute-done.18 = bf16[2,2,128,256]{3,2,1,0:T(8,128)(2,1)S(1)} collective-permute-done((bf16[2,2,128,256]{3,2,1,0:T(8,128)(2,1)S(1)}, bf16[2,2,128,256]{3,2,1,0:T(8,128)(2,1)S(1)}, u32[]{:S(2)}, u32[]{:S(2)}) %collective-permute-start.18) | collective-permute-done | bytes 262176 | tf_op jit(solution)/shard_map/ppermute | solution.py:19
  (151 shorter events, 55.6 us)
Async XLA Ops:
  0.6 25.2 %copy-start.7 = (bf16[1,128,4096]{2,1,0:T(8,128)(2,1)S(1)}, bf16[1,128,4096]{2,1,0:T(8,128)(2,1)}, u32[]{:S(2)}) copy-start(bf16[1,128,4096]{2,1,0:T(8,128)(2,1)} %param.7) | copy-start | bytes 3145732
  0.6 26.2 %copy-start.12 = (f32[4096]{0:T(1024)S(1)}, f32[4096]{0:T(1024)}, u32[]{:S(2)}) copy-start(f32[4096]{0:T(1024)} %param.8) | copy-start | bytes 49156
  0.7 25.2 %collective-permute-start.3 = (bf16[128,4096]{1,0:T(8,128)(2,1)}, bf16[128,4096]{1,0:T(8,128)(2,1)S(1)}, u32[]{:S(2)}, u32[]{:S(2)}) collective-permute-start(bf16[128,4096]{1,0:T(8,128)(2,1)} %bitcast.201), channel_id=1, source_target_pairs={{0,128},{128,0},{1,129},{129,1},{2,130},{130,2},{3,131},{131,3},{4... | collective-permute-start | bytes 3145736 | tf_op jit(solution)/shard_map/ppermute | solution.py:19
  2.6 9.3 collective-permute-start.7
  13.0 20.1 %collective-permute-start.8 = (bf16[512,768]{1,0:T(8,128)(2,1)S(1)}, bf16[512,768]{1,0:T(8,128)(2,1)}, u32[]{:S(2)}, u32[]{:S(2)}) collective-permute-start(bf16[512,768]{1,0:T(8,128)(2,1)S(1)} %bitcast.202), channel_id=1, source_target_pairs={{0,16},{1,17},{2,18},{3,19},{4,20},{5,21},{6,22},{7,23},{8,24},{9,... | collective-permute-start | bytes 2359304 | tf_op jit(solution)/shard_map/ppermute | solution.py:19
  25.8 1.0 copy-start.8
  28.5 6.0 copy-start.6
  28.5 7.7 collective-permute-start.4
  34.5 34.6 %collective-permute-start.9 = (bf16[1024,768]{1,0:T(8,128)(2,1)S(1)}, bf16[1024,768]{1,0:T(8,128)(2,1)}, u32[]{:S(2)}, u32[]{:S(2)}) collective-permute-start(bf16[1024,768]{1,0:T(8,128)(2,1)S(1)} %bitcast.198), channel_id=1, source_target_pairs={{0,32},{1,33},{2,34},{3,35},{4,36},{5,37},{6,38},{7,39},{8,40},{9,... | collective-permute-start | bytes 4718600 | tf_op jit(solution)/shard_map/ppermute | solution.py:19
  37.8 1.0 copy-start.3
  40.3 91.4 %collective-permute-start.5 = (bf16[2,128,4096]{2,1,0:T(8,128)(2,1)}, bf16[2,128,4096]{2,1,0:T(8,128)(2,1)}, u32[]{:S(2)}, u32[]{:S(2)}) collective-permute-start(bf16[2,128,4096]{2,1,0:T(8,128)(2,1)} %pad_maximum_fusion.4), channel_id=1, source_target_pairs={{0,2},{1,3},{2,0},{3,1},{4,6},{5,7},{6,4},{7,5},{8,10},{9,11},{10,... | collective-permute-start | bytes 6291464 | tf_op jit(solution)/shard_map/ppermute | solution.py:19
  70.7 61.1 %copy-start.4 = (bf16[1,128,4096]{2,1,0:T(8,128)(2,1)S(1)}, bf16[1,128,4096]{2,1,0:T(8,128)(2,1)}, u32[]{:S(2)}) copy-start(bf16[1,128,4096]{2,1,0:T(8,128)(2,1)} %copy-done.3) | copy-start | bytes 3145732
  72.6 599.5 %collective-permute-start.10 = (bf16[2048,768]{1,0:T(8,128)(2,1)}, bf16[2048,768]{1,0:T(8,128)(2,1)}, u32[]{:S(2)}, u32[]{:S(2)}) collective-permute-start(bf16[2048,768]{1,0:T(8,128)(2,1)} %bitcast.32), channel_id=1, source_target_pairs={{0,64},{1,65},{2,66},{3,67},{4,68},{5,69},{6,70},{7,71},{8,72},{9,... | collective-permute-start | bytes 9437192 | tf_op jit(solution)/shard_map/ppermute | solution.py:19
  133.7 2.6 copy-start.1
  133.8 7.2 copy-start.14
  136.4 542.2 %collective-permute-start.6 = (bf16[2,2,128,4096]{3,2,1,0:T(8,128)(2,1)}, bf16[2,2,128,4096]{3,2,1,0:T(8,128)(2,1)}, u32[]{:S(2)}, u32[]{:S(2)}) collective-permute-start(bf16[2,2,128,4096]{3,2,1,0:T(8,128)(2,1)} %pad_maximum_fusion.2), channel_id=1, source_target_pairs={{0,4},{1,5},{2,6},{3,7},{4,0},{5,1},{6,2},{7,3},{8,12},{9,13},{10,... | collective-permute-start | bytes 12582920 | tf_op jit(solution)/shard_map/ppermute | solution.py:19
  655.9 2.0 collective-permute-start
  656.0 0.5 copy-start.13
  657.9 4.6 collective-permute-start.1
  662.5 7.8 collective-permute-start.2
  675.4 3.2 copy-start.2
  683.8 7.6 copy-start.5
  691.4 11.3 copy-start
  705.0 687.0 %copy-start.9 = (f32[1024,768]{0,1:T(8,128)S(1)}, f32[1024,768]{0,1:T(8,128)}, u32[]{:S(2)}) copy-start(f32[1024,768]{0,1:T(8,128)} %fusion.60) | copy-start | bytes 9437188
  1394.9 3.6 copy-start.10
  1396.4 14.7 collective-permute-start.11
  1409.4 1.6 copy-start.11
  1471.5 2.0 collective-permute-start.12
  1474.8 21.7 %collective-permute-start.13 = (bf16[2,2,128,512]{3,2,1,0:T(8,128)(2,1)S(1)}, bf16[2,2,128,512]{3,2,1,0:T(8,128)(2,1)S(1)}, u32[]{:S(2)}, u32[]{:S(2)}) collective-permute-start(bf16[2,2,128,512]{3,2,1,0:T(8,128)(2,1)S(1)} %bitcast.206), channel_id=1, source_target_pairs={{0,2},{1,3},{2,0},{3,1},{4,6},{5,7},{6,4},{7,5},{8,10},{9,11},{10,... | collective-permute-start | bytes 1572872 | tf_op jit(solution)/shard_map/ppermute | solution.py:19
  1478.8 18.4 %collective-permute-start.16 = (bf16[2,2,128,256]{3,2,1,0:T(8,128)(2,1)}, bf16[2,2,128,256]{3,2,1,0:T(8,128)(2,1)}, u32[]{:S(2)}, u32[]{:S(2)}) collective-permute-start(bf16[2,2,128,256]{3,2,1,0:T(8,128)(2,1)} %bitcast.54), channel_id=1, source_target_pairs={{0,1},{1,0},{2,3},{3,2},{4,5},{5,4},{6,7},{7,6},{8,9},{9,8},{10,11... | collective-permute-start | bytes 786440 | tf_op jit(solution)/shard_map/ppermute | solution.py:19
  1496.6 24.7 %collective-permute-start.14 = (bf16[2,2,128,512]{3,2,1,0:T(8,128)(2,1)S(1)}, bf16[2,2,128,512]{3,2,1,0:T(8,128)(2,1)S(1)}, u32[]{:S(2)}, u32[]{:S(2)}) collective-permute-start(bf16[2,2,128,512]{3,2,1,0:T(8,128)(2,1)S(1)} %fusion.31), channel_id=1, source_target_pairs={{0,4},{1,5},{2,6},{3,7},{4,0},{5,1},{6,2},{7,3},{8,12},{9,13},{10,... | collective-permute-start | bytes 1572872 | tf_op jit(solution)/shard_map/ppermute | solution.py:19
  1499.0 34.4 %collective-permute-start.17 = (bf16[2,2,128,256]{3,2,1,0:T(8,128)(2,1)}, bf16[2,2,128,256]{3,2,1,0:T(8,128)(2,1)}, u32[]{:S(2)}, u32[]{:S(2)}) collective-permute-start(bf16[2,2,128,256]{3,2,1,0:T(8,128)(2,1)} %bitcast.175), channel_id=1, source_target_pairs={{0,2},{1,3},{2,0},{3,1},{4,6},{5,7},{6,4},{7,5},{8,10},{9,11},{10,... | collective-permute-start | bytes 786440 | tf_op jit(solution)/shard_map/ppermute | solution.py:19
  1522.8 47.2 %collective-permute-start.15 = (bf16[128,4096]{1,0:T(8,128)(2,1)S(1)}, bf16[128,4096]{1,0:T(8,128)(2,1)S(1)}, u32[]{:S(2)}, u32[]{:S(2)}) collective-permute-start(bf16[128,4096]{1,0:T(8,128)(2,1)S(1)} %copy.230), channel_id=1, source_target_pairs={{0,128},{128,0},{1,129},{129,1},{2,130},{130,2},{3,131},{131,3},{4... | collective-permute-start | bytes 3145736 | tf_op jit(solution)/shard_map/ppermute | solution.py:19
  1534.4 34.5 %collective-permute-start.18 = (bf16[2,2,128,256]{3,2,1,0:T(8,128)(2,1)S(1)}, bf16[2,2,128,256]{3,2,1,0:T(8,128)(2,1)S(1)}, u32[]{:S(2)}, u32[]{:S(2)}) collective-permute-start(bf16[2,2,128,256]{3,2,1,0:T(8,128)(2,1)S(1)} %fusion.41), channel_id=1, source_target_pairs={{0,4},{1,5},{2,6},{3,7},{4,0},{5,1},{6,2},{7,3},{8,12},{9,13},{10,... | collective-permute-start | bytes 786440 | tf_op jit(solution)/shard_map/ppermute | solution.py:19
where the time goes:
time: 1570 us
  blocking collectives  1200 us (76%)
  waiting for transfers between devices  189 us (12%)
  other arithmetic  68.4 us (4%)
  matrix products  43.1 us (3%)
  starting transfers between devices  33.6 us (2%)
  local copies, waits for them, and re-layouts  29.9 us (2%)
    psum x1, blocking collectives, body(): sink_table = lax.psum(slice_rows, 'tensor')  684 us
    psum x1, blocking collectives, body(): lax.psum(jnp.sum(segment_match.astype(jnp.float32), 0), 'tensor')  513 us
    ppermute x18, waiting for transfers between devices, from_partner(): return lax.ppermute(value, axis, pairs)  189 us
    another operation x30, other arithmetic, stack_pair(): return jnp.stack((lower_part, upper_part), axis=axis_pos)  37.3 us
    ppermute x18, starting transfers between devices, from_partner(): return lax.ppermute(value, axis, pairs)  31.5 us
  transfers between devices with their start and end apart: 19, of which 12 were waited for; matrix products, arithmetic and copies ran while one was open for 3% of the time, Pallas kernels for 0%

commit v1 on v0

--- a/solution.py
+++ b/solution.py
@@ -118,7 +118,7 @@
     slice_width = model_width // KEY_VALUE_HEADS
     own_slice = jnp.arange(model_width) // slice_width == head_number
     slice_rows = jnp.where(own_slice[None, :], selected_rows, 0.0)
-    sink_table = lax.psum(slice_rows, "tensor")
+    sink_table = jnp.sum(lax.all_gather(slice_rows, "tensor"), axis=0)
     sink_normed = sink_table.astype(jnp.bfloat16)
     sink_projected = jnp.dot(
         sink_normed,

time: 1570 us -> 1210 us (0.77)
  blocking collectives: 1200 us -> 514 us
  waiting for transfers between devices: 189 us -> 483 us
    psum x1 -> x0, blocking collectives: 684 us -> none  [body(): sink_table = lax.psum(slice_rows, 'tensor')]
    all_gather x0 -> x1, waiting for transfers between devices: none -> 148 us  [body(): sink_table = jnp.sum(lax.all_gather(slice_rows, 'tensor'), axis=0)]
    ppermute x18, waiting for transfers between devices: 189 us -> 319 us  [from_partner(): return lax.ppermute(value, axis, pairs)]
    reduce_sum x0 -> x1, other arithmetic: none -> 20.9 us  [body(): sink_table = jnp.sum(lax.all_gather(slice_rows, 'tensor'), axis=0)]
  transfers between devices with their start and end apart: 19 -> 20, of which waited for: 12 -> 17; matrix products, arithmetic and copies ran while one was open for 3% -> 3% of each run, Pallas kernels for 0% -> 0%
where the time goes in v1:
time: 1210 us; the launch traced here: 1200 us
  blocking collectives  514 us (42%)
  waiting for transfers between devices  483 us (40%)
  other arithmetic  73 us (6%)
  starting transfers between devices  41.8 us (3%)
  matrix products  34.7 us (3%)
  local copies, waits for them, and re-layouts  25.6 us (2%)
  between operations  15.4 us (1%)
    psum x1, blocking collectives, body(): lax.psum(jnp.sum(segment_match.astype(jnp.float32), 0), 'tensor')  514 us
    ppermute x18, waiting for transfers between devices, from_partner(): return lax.ppermute(value, axis, pairs)  319 us
    all_gather x1, waiting for transfers between devices, body(): sink_table = jnp.sum(lax.all_gather(slice_rows, 'tensor'), axis=0)  148 us
    ppermute x18, starting transfers between devices, from_partner(): return lax.ppermute(value, axis, pairs)  38.5 us
    another operation x30, other arithmetic, stack_pair(): return jnp.stack((lower_part, upper_part), axis=axis_pos)  29.5 us
  transfers between devices with their start and end apart: 20, of which 17 were waited for; matrix products, arithmetic and copies ran while one was open for 3% of the time, Pallas kernels for 0%

profile of v1, /device:TPU:32, one launch (start us, length us, event | category | flops | bytes accessed | tf_op | source)
XLA Modules:
  0.0 1195.5 jit_solution(7937454670775591132)
XLA Ops:
  7.2 1.9 collective-permute-start.3
  11.1 21.3 %collective-permute-done.3 = bf16[128,4096]{1,0:T(8,128)(2,1)S(1)} collective-permute-done((bf16[128,4096]{1,0:T(8,128)(2,1)}, bf16[128,4096]{1,0:T(8,128)(2,1)S(1)}, u32[]{:S(2)}, u32[]{:S(2)}) %collective-permute-start.3) | collective-permute-done | bytes 1048608 | tf_op jit(solution)/shard_map/ppermute | solution.py:19
  34.1 1.7 fusion.25
  35.8 2.6 collective-permute-done.4
  39.8 3.4 collective-permute-start.5
  43.1 89.9 %collective-permute-done.5 = bf16[2,128,4096]{2,1,0:T(8,128)(2,1)} collective-permute-done((bf16[2,128,4096]{2,1,0:T(8,128)(2,1)S(1)}, bf16[2,128,4096]{2,1,0:T(8,128)(2,1)}, u32[]{:S(2)}, u32[]{:S(2)}) %collective-permute-start.5) | collective-permute-done | bytes 2097184 | tf_op jit(solution)/shard_map/ppermute | solution.py:19
  133.0 2.1 select_bitcast_fusion.5
  135.1 2.6 pad_maximum_fusion.2
  137.8 4.8 collective-permute-start.6
  142.7 513.9 %psum.7 = f32[8]{0:T(128)S(1)} all-reduce(f32[8]{0:T(128)S(1)} %convert_reduce_fusion), channel_id=1, replica_groups=mesh['dp'=2,'tensor'=128] {'tensor'}, use_global_device_ids=true, to_apply=%region_3.4 | all-reduce | flops 8 | bytes 64 | tf_op jit(solution)/shard_map/psum | solution.py:72
  656.9 5.5 select_bitcast_fusion.1
  662.4 7.5 pad_maximum_fusion
  669.9 5.7 convolution_select_fusion
  675.7 14.8 %collective-permute-done.7 = bf16[256,768]{1,0:T(8,128)(2,1)S(1)} collective-permute-done((bf16[256,768]{1,0:T(8,128)(2,1)S(1)}, bf16[256,768]{1,0:T(8,128)(2,1)S(1)}, u32[]{:S(2)}, u32[]{:S(2)}) %collective-permute-start.7) | collective-permute-done | bytes 393248 | tf_op jit(solution)/shard_map/ppermute | solution.py:19
  690.8 14.6 %collective-permute-done.8 = bf16[512,768]{1,0:T(8,128)(2,1)S(1)} collective-permute-done((bf16[512,768]{1,0:T(8,128)(2,1)S(1)}, bf16[512,768]{1,0:T(8,128)(2,1)S(1)}, u32[]{:S(2)}, u32[]{:S(2)}) %collective-permute-start.8) | collective-permute-done | bytes 786464 | tf_op jit(solution)/shard_map/ppermute | solution.py:19
  705.8 54.8 %collective-permute-done.9 = bf16[1024,768]{1,0:T(8,128)(2,1)S(1)} collective-permute-done((bf16[1024,768]{1,0:T(8,128)(2,1)S(1)}, bf16[1024,768]{1,0:T(8,128)(2,1)S(1)}, u32[]{:S(2)}, u32[]{:S(2)}) %collective-permute-start.9) | collective-permute-done | bytes 1572896 | tf_op jit(solution)/shard_map/ppermute | solution.py:19
  763.5 3.7 collective-permute-done.1
  768.3 7.0 collective-permute-done.2
  775.3 41.2 %collective-permute-done.10 = bf16[2048,768]{1,0:T(8,128)(2,1)} collective-permute-done((bf16[2048,768]{1,0:T(8,128)(2,1)S(1)}, bf16[2048,768]{1,0:T(8,128)(2,1)}, u32[]{:S(2)}, u32[]{:S(2)}) %collective-permute-start.10) | collective-permute-done | bytes 3145760 | tf_op jit(solution)/shard_map/ppermute | solution.py:19
  816.5 4.2 select_bitcast_fusion.3
  820.7 2.6 pad_maximum_fusion.1
  823.9 7.0 fusion.60
  832.9 1.8 copy.243
  834.7 2.0 copy.242
  836.7 2.8 subtract_convert_fusion.1
  841.8 3.2 collective-permute-start.11
  845.0 2.1 subtract_convert_fusion
  848.8 15.4 %collective-permute-done.11 = bf16[1024,256]{0,1:T(8,128)(2,1)S(1)} collective-permute-done((bf16[1024,256]{0,1:T(8,128)(2,1)S(1)}, bf16[1024,256]{0,1:T(8,128)(2,1)S(1)}, u32[]{:S(2)}, u32[]{:S(2)}) %collective-permute-start.11) | collective-permute-done | bytes 524320 | tf_op jit(solution)/shard_map/ppermute | solution.py:25
  865.3 148.4 %all-gather.3.cloned.1.call-done = f32[4096,4096]{1,0:T(8,128)} async-done(((f32[32,4096]{1,0:T(8,128)}), f32[4096,4096]{1,0:T(8,128)}) %all-gather.3.cloned.1.call-update) | async-done | bytes 67108880 | tf_op jit(solution)/shard_map/all_gather | solution.py:121
  1013.7 20.9 %reduce_sum.81 = bf16[32,4096]{1,0:T(8,128)(2,1)S(1)} reduce(f32[128,32,4096]{2,1,0:T(8,128)} %bitcast.37, f32[]{:T(128)} %constant.196.clone.1), dimensions={0}, to_apply=%region_6.7 | reduce | flops 16646144 | bytes 67371008 | tf_op jit(solution)/shard_map/reduce_sum | solution.py:121
  1034.5 2.1 fusion.26
  1036.8 44.2 %while.15 = (s32[]{:T(128)}, bf16[2,512,512]{2,1,0:T(8,128)(2,1)}, s32[2]{0:T(128)S(1)}, s32[]{:T(128)}, s32[]{:T(128)}, /*index=5*/s32[1024]{0:T(1024)S(1)}, bf...) while((s32[]{:T(128)}, bf16[2,512,512]{2,1,0:T(8,128)(2,1)}, ...), condition=%wide.region_12.13_spmd, body=%wide.region_7.12_spmd.sunk | while | flops 1115269120 | bytes 74897784 | solution.py:202
  1045.1 2.7 fusion.93
  1047.9 2.4 fusion.96
  1052.7 5.2 fusion.99
  1067.3 2.7 fusion.93
  1070.1 2.4 fusion.96
  1074.8 5.2 fusion.99
  1082.5 1.7 collective-permute-done.12
  1085.5 2.8 collective-permute-start.13
  1090.9 20.2 %collective-permute-done.13 = bf16[2,2,128,512]{3,2,1,0:T(8,128)(2,1)S(1)} collective-permute-done((bf16[2,2,128,512]{3,2,1,0:T(8,128)(2,1)S(1)}, bf16[2,2,128,512]{3,2,1,0:T(8,128)(2,1)S(1)}, u32[]{:S(2)}, u32[]{:S(2)}) %collective-permute-start.13) | collective-permute-done | bytes 524320 | tf_op jit(solution)/shard_map/ppermute | solution.py:19
  1111.3 3.6 collective-permute-start.14
  1117.2 3.4 collective-permute-start.17
  1120.5 8.9 collective-permute-done.14
  1130.9 13.7 %collective-permute-start.15 = (bf16[128,4096]{1,0:T(8,128)(2,1)S(1)}, bf16[128,4096]{1,0:T(8,128)(2,1)S(1)}, u32[]{:S(2)}, u32[]{:S(2)}) collective-permute-start(bf16[128,4096]{1,0:T(8,128)(2,1)S(1)} %copy.230), channel_id=1, source_target_pairs={{0,128},{128,0},{1,129},{129,1},{2,130},{130,2},{3,131},{131,3},{4... | collective-permute-start | bytes 3145736 | tf_op jit(solution)/shard_map/ppermute | solution.py:19
  1144.6 4.8 collective-permute-done.17
  1150.5 3.5 collective-permute-start.18
  1154.0 32.4 %collective-permute-done.18 = bf16[2,2,128,256]{3,2,1,0:T(8,128)(2,1)S(1)} collective-permute-done((bf16[2,2,128,256]{3,2,1,0:T(8,128)(2,1)S(1)}, bf16[2,2,128,256]{3,2,1,0:T(8,128)(2,1)S(1)}, u32[]{:S(2)}, u32[]{:S(2)}) %collective-permute-start.18) | collective-permute-done | bytes 262176 | tf_op jit(solution)/shard_map/ppermute | solution.py:19
  (161 shorter events, 44.7 us)
Async XLA Ops:
  7.2 1006.5 %all-gather.3.cloned.1.call-start = ((), (), s32[]{:S(2)}) async-start(), calls=%async_computation | async-start | bytes 67633152 | tf_op jit(solution)/shard_map/all_gather | solution.py:121
  7.2 25.2 %collective-permute-start.3 = (bf16[128,4096]{1,0:T(8,128)(2,1)}, bf16[128,4096]{1,0:T(8,128)(2,1)S(1)}, u32[]{:S(2)}, u32[]{:S(2)}) collective-permute-start(bf16[128,4096]{1,0:T(8,128)(2,1)} %bitcast.205), channel_id=1, source_target_pairs={{0,128},{128,0},{1,129},{129,1},{2,130},{130,2},{3,131},{131,3},{4... | collective-permute-start | bytes 3145736 | tf_op jit(solution)/shard_map/ppermute | solution.py:19
  35.7 2.7 collective-permute-start.4
  38.6 1.0 copy-start.2
  39.8 93.2 %collective-permute-start.5 = (bf16[2,128,4096]{2,1,0:T(8,128)(2,1)S(1)}, bf16[2,128,4096]{2,1,0:T(8,128)(2,1)}, u32[]{:S(2)}, u32[]{:S(2)}) collective-permute-start(bf16[2,128,4096]{2,1,0:T(8,128)(2,1)S(1)} %pad_maximum_fusion.4), channel_id=1, source_target_pairs={{0,2},{1,3},{2,0},{3,1},{4,6},{5,7},{6,4},{7,5},{8,10},{9,11},{10,... | collective-permute-start | bytes 6291464 | tf_op jit(solution)/shard_map/ppermute | solution.py:19
  135.1 2.7 copy-start.1
  135.1 7.4 copy-start.13
  137.8 519.1 %collective-permute-start.6 = (bf16[2,2,128,4096]{3,2,1,0:T(8,128)(2,1)}, bf16[2,2,128,4096]{3,2,1,0:T(8,128)(2,1)}, u32[]{:S(2)}, u32[]{:S(2)}) collective-permute-start(bf16[2,2,128,4096]{3,2,1,0:T(8,128)(2,1)} %pad_maximum_fusion.2), channel_id=1, source_target_pairs={{0,4},{1,5},{2,6},{3,7},{4,0},{5,1},{6,2},{7,3},{8,12},{9,13},{10,... | collective-permute-start | bytes 12582920 | tf_op jit(solution)/shard_map/ppermute | solution.py:19
  669.9 5.8 copy-start.8
  675.6 14.9 %collective-permute-start.7 = (bf16[256,768]{1,0:T(8,128)(2,1)S(1)}, bf16[256,768]{1,0:T(8,128)(2,1)S(1)}, u32[]{:S(2)}, u32[]{:S(2)}) collective-permute-start(bf16[256,768]{1,0:T(8,128)(2,1)S(1)} %copy-done.8), channel_id=1, source_target_pairs={{0,8},{1,9},{2,10},{3,11},{4,12},{5,13},{6,14},{7,15},{8,0},{9,1},... | collective-permute-start | bytes 1179656 | tf_op jit(solution)/shard_map/ppermute | solution.py:19
  690.7 14.7 %collective-permute-start.8 = (bf16[512,768]{1,0:T(8,128)(2,1)S(1)}, bf16[512,768]{1,0:T(8,128)(2,1)S(1)}, u32[]{:S(2)}, u32[]{:S(2)}) collective-permute-start(bf16[512,768]{1,0:T(8,128)(2,1)S(1)} %bitcast.206), channel_id=1, source_target_pairs={{0,16},{1,17},{2,18},{3,19},{4,20},{5,21},{6,22},{7,23},{8,24},{9,... | collective-permute-start | bytes 2359304 | tf_op jit(solution)/shard_map/ppermute | solution.py:19
  705.7 54.9 %collective-permute-start.9 = (bf16[1024,768]{1,0:T(8,128)(2,1)S(1)}, bf16[1024,768]{1,0:T(8,128)(2,1)S(1)}, u32[]{:S(2)}, u32[]{:S(2)}) collective-permute-start(bf16[1024,768]{1,0:T(8,128)(2,1)S(1)} %bitcast.202), channel_id=1, source_target_pairs={{0,32},{1,33},{2,34},{3,35},{4,36},{5,37},{6,38},{7,39},{8,40},{9,... | collective-permute-start | bytes 4718600 | tf_op jit(solution)/shard_map/ppermute | solution.py:19
  761.3 55.3 %collective-permute-start.10 = (bf16[2048,768]{1,0:T(8,128)(2,1)S(1)}, bf16[2048,768]{1,0:T(8,128)(2,1)}, u32[]{:S(2)}, u32[]{:S(2)}) collective-permute-start(bf16[2048,768]{1,0:T(8,128)(2,1)S(1)} %bitcast.198), channel_id=1, source_target_pairs={{0,64},{1,65},{2,66},{3,67},{4,68},{5,69},{6,70},{7,71},{8,72},{9,... | collective-permute-start | bytes 9437192 | tf_op jit(solution)/shard_map/ppermute | solution.py:19
  761.4 1.2 collective-permute-start
  761.5 2.0 copy-start.11
  762.6 4.6 collective-permute-start.1
  767.2 8.0 collective-permute-start.2
  816.5 6.9 slice-start
  820.7 3.1 slice-start.1
  823.4 7.5 copy-start.3
  830.9 2.0 copy-start.4
  832.9 3.8 copy-start.12
  841.8 5.4 copy-start.5
  841.8 22.4 %collective-permute-start.11 = (bf16[1024,256]{0,1:T(8,128)(2,1)S(1)}, bf16[1024,256]{0,1:T(8,128)(2,1)S(1)}, u32[]{:S(2)}, u32[]{:S(2)}) collective-permute-start(bf16[1024,256]{0,1:T(8,128)(2,1)S(1)} %pad_maximum_fusion.9), channel_id=1, source_target_pairs={{0,8},{1,9},{2,10},{3,11},{4,12},{5,13},{6,14},{7,15},{8,16},{9,17... | collective-permute-start | bytes 1572872 | tf_op jit(solution)/shard_map/ppermute | solution.py:25
  847.2 17.1 %copy-start.7 = (bf16[1024,64]{0,1:T(8,128)(2,1)S(1)}, bf16[1024,64]{0,1:T(8,128)(2,1)}, u32[]{:S(2)}) copy-start(bf16[1024,64]{0,1:T(8,128)(2,1)} %get-tuple-element.360) | copy-start | bytes 393220
  1013.7 23.0 %copy-start.9 = (f32[4,64]{1,0:T(4,128)S(1)}, f32[4,64]{1,0:T(4,128)}, u32[]{:S(2)}) copy-start(f32[4,64]{1,0:T(4,128)} %get-tuple-element.401) | copy-start | bytes 3076
  1013.7 23.1 %copy-start.10 = (f32[4,64]{1,0:T(4,128)S(1)}, f32[4,64]{1,0:T(4,128)}, u32[]{:S(2)}) copy-start(f32[4,64]{1,0:T(4,128)} %get-tuple-element.402) | copy-start | bytes 3076
  1013.7 23.2 %copy-start.14 = (s32[2]{0:T(128)S(1)}, s32[2]{0:T(128)}, u32[]{:S(2)}) copy-start(s32[2]{0:T(128)} %iota_multiply_fusion) | copy-start | bytes 28
  1047.9 3.3 copy-start
  1070.0 3.3 copy-start
  1081.1 7.3 copy-start.6
  1082.2 2.0 collective-permute-start.12
  1085.5 25.7 %collective-permute-start.13 = (bf16[2,2,128,512]{3,2,1,0:T(8,128)(2,1)S(1)}, bf16[2,2,128,512]{3,2,1,0:T(8,128)(2,1)S(1)}, u32[]{:S(2)}, u32[]{:S(2)}) collective-permute-start(bf16[2,2,128,512]{3,2,1,0:T(8,128)(2,1)S(1)} %bitcast.210), channel_id=1, source_target_pairs={{0,2},{1,3},{2,0},{3,1},{4,6},{5,7},{6,4},{7,5},{8,10},{9,11},{10,... | collective-permute-start | bytes 1572872 | tf_op jit(solution)/shard_map/ppermute | solution.py:19
  1090.9 24.5 %collective-permute-start.16 = (bf16[2,2,128,256]{3,2,1,0:T(8,128)(2,1)}, bf16[2,2,128,256]{3,2,1,0:T(8,128)(2,1)}, u32[]{:S(2)}, u32[]{:S(2)}) collective-permute-start(bf16[2,2,128,256]{3,2,1,0:T(8,128)(2,1)} %bitcast.55), channel_id=1, source_target_pairs={{0,1},{1,0},{2,3},{3,2},{4,5},{5,4},{6,7},{7,6},{8,9},{9,8},{10,11... | collective-permute-start | bytes 786440 | tf_op jit(solution)/shard_map/ppermute | solution.py:19
  1111.3 18.2 %collective-permute-start.14 = (bf16[2,2,128,512]{3,2,1,0:T(8,128)(2,1)S(1)}, bf16[2,2,128,512]{3,2,1,0:T(8,128)(2,1)S(1)}, u32[]{:S(2)}, u32[]{:S(2)}) collective-permute-start(bf16[2,2,128,512]{3,2,1,0:T(8,128)(2,1)S(1)} %fusion.31), channel_id=1, source_target_pairs={{0,4},{1,5},{2,6},{3,7},{4,0},{5,1},{6,2},{7,3},{8,12},{9,13},{10,... | collective-permute-start | bytes 1572872 | tf_op jit(solution)/shard_map/ppermute | solution.py:19
  1117.2 32.3 %collective-permute-start.17 = (bf16[2,2,128,256]{3,2,1,0:T(8,128)(2,1)}, bf16[2,2,128,256]{3,2,1,0:T(8,128)(2,1)}, u32[]{:S(2)}, u32[]{:S(2)}) collective-permute-start(bf16[2,2,128,256]{3,2,1,0:T(8,128)(2,1)} %bitcast.176), channel_id=1, source_target_pairs={{0,2},{1,3},{2,0},{3,1},{4,6},{5,7},{6,4},{7,5},{8,10},{9,11},{10,... | collective-permute-start | bytes 786440 | tf_op jit(solution)/shard_map/ppermute | solution.py:19
  1130.9 56.5 %collective-permute-start.15 = (bf16[128,4096]{1,0:T(8,128)(2,1)S(1)}, bf16[128,4096]{1,0:T(8,128)(2,1)S(1)}, u32[]{:S(2)}, u32[]{:S(2)}) collective-permute-start(bf16[128,4096]{1,0:T(8,128)(2,1)S(1)} %copy.230), channel_id=1, source_target_pairs={{0,128},{128,0},{1,129},{129,1},{2,130},{130,2},{3,131},{131,3},{4... | collective-permute-start | bytes 3145736 | tf_op jit(solution)/shard_map/ppermute | solution.py:19
  1150.5 35.9 %collective-permute-start.18 = (bf16[2,2,128,256]{3,2,1,0:T(8,128)(2,1)S(1)}, bf16[2,2,128,256]{3,2,1,0:T(8,128)(2,1)S(1)}, u32[]{:S(2)}, u32[]{:S(2)}) collective-permute-start(bf16[2,2,128,256]{3,2,1,0:T(8,128)(2,1)S(1)} %fusion.41), channel_id=1, source_target_pairs={{0,4},{1,5},{2,6},{3,7},{4,0},{5,1},{6,2},{7,3},{8,12},{9,13},{10,... | collective-permute-start | bytes 786440 | tf_op jit(solution)/shard_map/ppermute | solution.py:19
Sparse Core Ops, SparseCore 0:
  675.7 337.8 all-gather.2
